TPU v7x, 128 devices: a whole 4x4x4 slice. The times are simulated.
128 devices in a mesh: img: 32 (over x, y, core), tok: 4 (over z).
Axes of the slice: x: 4, y: 4, z: 4, core: 2. Of those that a mesh axis runs over, the one named last changes fastest.
Arguments:
- tokens: bfloat16 [32, 4096, 1280], P('img', 'tok'), may hold values from -8 to 8
- ln_gain: float32 [1280], replicated, may hold values from 0.25 to 1.75
- w_qkv: bfloat16 [1280, 1920], replicated, may hold values from -2 to 2
- w_proj: bfloat16 [640, 1280], replicated, may hold values from -0.25 to 0.25
- w_neck1: bfloat16 [1280, 256], replicated, may hold values from -0.15625 to 0.15625
- neck_gain1: float32 [256], replicated, may hold values from 0.25 to 1.75
- w_neck2: bfloat16 [2304, 256], replicated, may hold values from -0.125 to 0.125
- neck_gain2: float32 [256], replicated, may hold values from 0.25 to 1.75
- pe_matrix: float32 [2, 128], replicated, may hold values from -6 to 6
- query_bias: float32 [256], replicated, may hold values from -6 to 6
- dec_qkv: float32 [3, 256, 128], replicated, may hold values from -2 to 2
- dec_out: float32 [128, 256], replicated, may hold values from -0.5 to 0.5
- dec_gains: float32 [2, 256], replicated, may hold values from 0.25 to 1.75
- w_mlp1: float32 [256, 2048], replicated, may hold values from -0.375 to 0.375
- w_mlp2: float32 [2048, 256], replicated, may hold values from -0.1875 to 0.1875
- w_hyper: float32 [2, 256, 256], replicated, may hold values from -0.5 to 0.5
- w_hyper_out: float32 [256, 32], replicated, may hold values from -0.5 to 0.5
- w_up1: float32 [256, 256], replicated, may hold values from -0.375 to 0.375
- up_gain: float32 [64], replicated, may hold values from 0.25 to 1.75
- w_up2: float32 [64, 128], replicated, may hold values from -0.75 to 0.75
- req_image: int32 [2048, 1], P('img'), may hold values from 0 to 31; in each aligned block of 64 rows (0 to 63, 64 to 127, ...) at most 4 rows name the same one
- points: int32 [2048, 2], P('img'), may hold values from 0 to 1023
Outputs:
- masks: float32 [2048, 65536], P('img', 'tok')
Inputs may be any that keep to these rules, and one draw needn't show every extreme that they name: `req_image`: among the 64 rows of one owner no image is named more than 4 times; in some owner's rows an image is named exactly 4 times.
All inputs are finite; a program needn't handle non-finite values.
Results may differ from a plain program's by a relative error of at most 0.035.
Values may be sent and summed in bfloat16 or wider, within the bound.
A program may use at most 320 MiB of HBM per device.

v0:
```python
import math

import jax
import jax.numpy as jnp
from jax import lax
from jax.experimental import pallas as pl
from jax.experimental.pallas import tpu as pltpu
from jax.sharding import PartitionSpec as P

HEADS = 8
HDIM = 80
GRID = 64
NECK = 256
ATTN_DIM = 128
DEC_HEADS = 8
UP1 = 64
UP2 = 32
IMG_SIDE = 1024
CAP = 4
RING = 4
MESH = pl.DeviceIdType.MESH
bf16 = jnp.bfloat16
f32 = jnp.float32
LOG2E = math.log2(math.e)
highest_precision = lax.Precision.HIGHEST


def norm_rows(x, gain, eps):
    centred = x - jnp.mean(x, axis=-1, keepdims=True)
    spread = jnp.mean(centred * centred, axis=-1, keepdims=True)
    return centred * lax.rsqrt(spread + eps) * gain


def iota(shape, axis):
    return lax.broadcasted_iota(jnp.int32, shape, axis)


def dot(a, b):
    return jnp.dot(a, b, preferred_element_type=f32)


def exact_dot(a, b):
    return jnp.dot(a, b, preferred_element_type=f32, precision=highest_precision)


def gelu(x):
    return 0.5 * x * (1.0 + lax.erf(x * math.sqrt(0.5)))


def request_places(targets, owners):
    count = targets.shape[1]
    match = (iota((owners, count), 0) == targets).astype(f32)
    earlier = (iota((count, count), 0) < iota((count, count), 1)).astype(bf16)
    seen = dot(match.astype(bf16), earlier)
    return targets, jnp.sum(seen * match, axis=0, keepdims=True).astype(jnp.int32)


def partner(img, k):
    dx, dy, dc = k // 8, (k // 2) % 4, k % 2
    x, y, core = img // 8, (img // 2) % 4, img % 2
    return lax.rem(x + dx, 4) * 8 + lax.rem(y + dy, 4) * 2 + lax.rem(core + dc, 2)


def split(x):
    high = x.astype(bf16)
    return high, (x - high.astype(f32)).astype(bf16)


def trunk_kernel(
    tok_hbm, gain_ref, wqkv_hbm, wproj_hbm, wn1_hbm, g1_ref, wn2_hbm, g2_ref,
    req_ref, points_ref, pe_ref, bias_ref, dec_qkv_ref, dec_out_ref, dec_gains_ref,
    mlp1_hbm, mlp2_hbm, hyper_hbm, hyper_out_ref, up1_ref, up_gain_ref, up2_ref,
    chosen_ref, mover_ref,
    tok, wqkv, wproj, wn1, wn2, normed, loc, got, vrows, outs, att, maps, halo,
    load_sem, qkv_send, qkv_recv, out_send, out_recv, halo_send, halo_recv,
    emb_ref, outgoing, arrived, mlp1, mlp2, hyper, keys, values, mixed, level, got_mixed, got_level, ups,
    ready, received, chooser,
    late_sem, point_send, point_recv, stat_send, stat_recv, mask_send, mask_recv,
):
    me = lax.axis_index("tok")
    rows = tok.shape[0]
    two = 2 * HDIM
    slots = received.shape[1] * CAP
    contract = (((1,), (1,)), ((), ()))
    inner = HEADS * HDIM
    tile = 256
    tiles = rows // tile
    qblock = 512

    loads = [
        pltpu.make_async_copy(tok_hbm.at[pl.ds(i * tile, tile)], tok.at[pl.ds(i * tile, tile)], load_sem.at[i])
        for i in range(tiles)
    ]
    loads.append(pltpu.make_async_copy(wqkv_hbm, wqkv, load_sem.at[4]))
    loads.append(pltpu.make_async_copy(wn1_hbm, wn1, load_sem.at[5]))
    loads.append(pltpu.make_async_copy(wn2_hbm, wn2, load_sem.at[6]))
    for d in range(RING):
        owner = lax.rem(me + d, RING)
        loads.append(
            pltpu.make_async_copy(
                wproj_hbm.at[pl.ds(pl.multiple_of(owner * two, 32), two)],
                wproj.at[pl.ds(d * two, two)],
                load_sem.at[7 + d],
            )
        )
    late = [
        pltpu.make_async_copy(a, b, late_sem.at[i])
        for i, (a, b) in enumerate(((mlp1_hbm, mlp1), (mlp2_hbm, mlp2), (hyper_hbm, hyper)))
    ]
    for load in loads + late:
        load.start()

    img = lax.axis_index("img")
    owners = received.shape[1]
    barrier = pltpu.get_barrier_semaphore()
    for d in range(1, RING):
        pl.semaphore_signal(
            barrier, inc=1, device_id={"tok": lax.rem(me + d, RING)}, device_id_type=MESH
        )

    @pl.loop(1, owners)
    def _(k):
        pl.semaphore_signal(barrier, inc=1, device_id={"img": partner(img, k)}, device_id_type=MESH)

    for i in range(tiles):
        loads[i].wait()
        span = pl.ds(i * tile, tile)
        normed[span, :] = norm_rows(tok[span, :].astype(f32), gain_ref[...], 1e-06).astype(bf16)
    loads[4].wait()

    scale = math.log2(math.e) / math.sqrt(HDIM)

    def qkv_copy(kind, head, d):
        owner = lax.rem(me + d, RING)
        first = pl.multiple_of(kind * inner + owner * two + head * HDIM, 16)
        return pltpu.make_async_remote_copy(
            src_ref=loc.at[pl.ds(first, HDIM)],
            dst_ref=got.at[kind, head, d],
            send_sem=qkv_send.at[kind, head, d],
            recv_sem=qkv_recv.at[kind, head, d],
            device_id={"tok": owner},
            device_id_type=MESH,
        )

    def project(kind):
        @pl.loop(0, tiles)
        def _(i):
            span = pl.ds(pl.multiple_of(i * tile, tile), tile)
            part = jnp.dot(
                normed[span, :], wqkv[:, kind * inner : (kind + 1) * inner], preferred_element_type=f32
            )
            if kind == 0:
                part = part * scale
            loc[kind * inner : (kind + 1) * inner, span] = part.astype(bf16).T

    for kind in (1, 2, 0):
        project(kind)
        if kind == 1:
            pl.semaphore_wait(barrier, owners - 1 + RING - 1)
        for d in (1, 3, 2):
            qkv_copy(kind, 0, d).start()
    for kind in (1, 2, 0):
        for d in (1, 3, 2):
            qkv_copy(kind, 1, d).start()
    place = request_places(req_ref[...], owners)
    placing = (iota((owners * 8, slots // 2), 0) == place[0] * 8 + place[1]).astype(bf16)
    line = iota((128, slots // 2), 0)
    across, down = points_ref[0:1, :], points_ref[1:2, :]
    parts = jnp.where(
        line == 0,
        across // 32,
        jnp.where(line == 1, across % 32, jnp.where(line == 2, down // 32, jnp.where(line == 3, down % 32, 0))),
    )
    outgoing[...] = lax.dot_general(
        placing, parts.astype(f32).astype(bf16), contract, preferred_element_type=f32
    ).reshape(owners, 8, 128)

    def point_copy(k):
        to = partner(img, k)
        return pltpu.make_async_remote_copy(
            src_ref=outgoing.at[to], dst_ref=arrived.at[img],
            send_sem=point_send.at[k], recv_sem=point_recv.at[k],
            device_id={"img": to}, device_id_type=MESH,
        )

    for kind in range(3):
        for head in range(2):
            first = pl.multiple_of(kind * inner + me * two + head * HDIM, 16)
            got[kind, head, 0] = loc[pl.ds(first, HDIM), :]

    @pl.loop(1, owners)
    def _(k):
        point_copy(k).start()
    arrived[img] = outgoing[img]

    def out_copy(head, d):
        target = lax.rem(me - d + RING, RING)
        return pltpu.make_async_remote_copy(
            src_ref=outs.at[head, d],
            dst_ref=att.at[d, pl.ds(pl.multiple_of(head * HDIM, 16), HDIM)],
            send_sem=out_send.at[head, d],
            recv_sem=out_recv.at[head, d],
            device_id={"tok": target},
            device_id_type=MESH,
        )

    filler = (lax.broadcasted_iota(jnp.int32, (48, rows), 0) == 0).astype(bf16)
    halves = rows // qblock

    @pl.loop(0, 2)
    def _(head):
        for d in range(1, RING):
            qkv_copy(1, head, d).wait_recv()
            qkv_copy(2, head, d).wait_recv()
        for d in range(RING):
            vrows[d] = jnp.concatenate([got[2, head, d], filler], axis=0).T

        @pl.loop(0, RING)
        def _(turn):
            slot = lax.rem(turn + head, RING)

            @pl.when(slot > 0)
            def _():
                qkv_copy(0, head, slot).wait_recv()

            @pl.loop(0, halves)
            def _(half):
                span = pl.ds(pl.multiple_of(half * qblock, qblock), qblock)
                query = got[0, head, slot, :, span].T

                def scores(d):
                    return jnp.dot(query, got[1, head, d], preferred_element_type=f32)

                now = scores(0)
                top = None
                for d in range(RING):
                    ahead = scores(d + 1) if d + 1 < RING else None
                    here = jnp.max(now, axis=1, keepdims=True)
                    fresh = here if top is None else jnp.maximum(top, here)
                    weights = jnp.exp2(now - fresh).astype(bf16)
                    part = jnp.dot(weights, vrows[d], preferred_element_type=f32)
                    total = part if top is None else total * jnp.exp2(top - fresh) + part
                    top, now = fresh, ahead
                final = (total * (1.0 / total[:, HDIM : HDIM + 1])).astype(bf16).T[:HDIM]
                outs[head, slot, :, span] = final

            @pl.when(slot > 0)
            def _():
                out_copy(head, slot).start()

            @pl.when(slot == 0)
            def _():
                att[0, pl.ds(pl.multiple_of(head * HDIM, 16), HDIM), :] = outs[head, 0]

    for d in range(1, RING):
        for head in range(2):
            out_copy(head, d).wait_recv()
    for load in loads[5:]:
        load.wait()

    def halo_copy(side):
        start = GRID + (0 if side == 0 else rows - GRID)
        return pltpu.make_async_remote_copy(
            src_ref=maps.at[1, pl.ds(start, GRID)],
            dst_ref=halo.at[side],
            send_sem=halo_send.at[side],
            recv_sem=halo_recv.at[side],
            device_id={"tok": lax.rem(me + (RING - 1 if side == 0 else 1), RING)},
            device_id_type=MESH,
        )

    def spread_columns(plain, at):
        count = plain.shape[0]
        column = lax.broadcasted_iota(jnp.int32, (count, NECK), 0) % GRID
        maps[1, at, :] = plain.astype(bf16)
        maps[0, at, :] = jnp.where(column == 0, 0.0, pltpu.roll(plain, 1, 0)).astype(bf16)
        maps[2, at, :] = jnp.where(column == GRID - 1, 0.0, pltpu.roll(plain, count - 1, 0)).astype(bf16)

    def narrow_tile(i):
        span = pl.ds(pl.multiple_of(i * tile, tile), tile)
        mixed = jnp.concatenate(
            [att[d, :, span] for d in range(RING)], axis=0
        ).T
        block = tok[span, :].astype(f32) + jnp.dot(mixed, wproj[...], preferred_element_type=f32)
        thin = jnp.dot(block.astype(bf16), wn1[...], preferred_element_type=f32)
        thin = norm_rows(thin, g1_ref[...], 1e-06).astype(bf16).astype(f32)
        spread_columns(thin, pl.ds(pl.multiple_of(GRID + i * tile, GRID), tile))

    @pl.loop(0, 2)
    def _(i):
        narrow_tile(i * (tiles - 1))
    halo_copy(0).start()
    halo_copy(1).start()
    @pl.loop(1, tiles - 1)
    def _(i):
        narrow_tile(i)

    def conv_tile(i):
        total = None
        for row_off in range(3):
            at = pl.ds(pl.multiple_of(i * tile + row_off * GRID, GRID), tile)
            for col_off in range(3):
                tap = (row_off * 3 + col_off) * NECK
                part = jnp.dot(maps[col_off, at, :], wn2[tap : tap + NECK, :], preferred_element_type=f32)
                total = part if total is None else total + part
        emb_ref[pl.ds(pl.multiple_of(i * tile, tile), tile), :] = norm_rows(
            total, g2_ref[...], 1e-06
        )

    @pl.loop(1, tiles - 1)
    def _(i):
        conv_tile(i)

    halo_copy(0).wait_recv()
    halo_copy(1).wait_recv()
    above = halo[1].astype(f32) * (me > 0).astype(f32)
    below = halo[0].astype(f32) * (me < RING - 1).astype(f32)
    spread_columns(above, pl.ds(0, GRID))
    spread_columns(below, pl.ds(GRID + rows, GRID))

    @pl.loop(0, 2)
    def _(i):
        conv_tile(i * (tiles - 1))

    for kind in range(3):
        for head in range(2):
            for d in range(1, RING):
                qkv_copy(kind, head, d).wait_send()
    for head in range(2):
        for d in range(1, RING):
            out_copy(head, d).wait_send()
    halo_copy(0).wait_send()
    halo_copy(1).wait_send()
    width = ATTN_DIM // DEC_HEADS
    turn = 2.0 * math.pi
    px_row, py_row = pe_ref[0:1, :], pe_ref[1:2, :]
    grid_rows = rows // GRID
    col_angle = turn * (((iota((GRID, 128), 0).astype(f32) + 0.5) / GRID * 2.0 - 1.0) * px_row)
    row_no = iota((grid_rows, 128), 0) + me * grid_rows
    row_angle = turn * (((row_no.astype(f32) + 0.5) / GRID * 2.0 - 1.0) * py_row)
    col_sin, col_cos = jnp.sin(col_angle), jnp.cos(col_angle)
    row_sin, row_cos = jnp.sin(row_angle), jnp.cos(row_angle)
    key_w = dec_qkv_ref[1]
    value_w = dec_qkv_ref[2].astype(bf16)
    key_high, key_low = split(key_w)
    for r in range(grid_rows):
        span = pl.ds(r * GRID, GRID)
        rs, rc = row_sin[r : r + 1], row_cos[r : r + 1]
        code = jnp.concatenate(
            [col_sin * rc + col_cos * rs, col_cos * rc - col_sin * rs], axis=1
        )
        cell = emb_ref[span, :]
        high, low = split(cell + code)
        projected = dot(high, key_high) + (dot(high, key_low) + dot(low, key_high))
        k_high, k_low = split(projected)
        keys[span, 0:128] = k_high
        keys[span, 128:256] = k_low
        values[span, :] = dot(cell.astype(bf16), value_w).astype(bf16)

    @pl.loop(1, owners)
    def _(k):
        point_copy(k).wait_recv()

    row = iota((slots, owners * 8), 0)
    pick = (iota((slots, owners * 8), 1) == (row // CAP) * 8 + row % CAP).astype(bf16)
    picked = dot(pick, arrived[...].reshape(owners * 8, 128).astype(bf16))
    where_x = picked[:, 0:1] * 32.0 + picked[:, 1:2]
    where_y = picked[:, 2:3] * 32.0 + picked[:, 3:4]
    angle = turn * (
        ((where_x + 0.5) / IMG_SIDE * 2.0 - 1.0) * px_row + ((where_y + 0.5) / IMG_SIDE * 2.0 - 1.0) * py_row
    )
    query_tok = bias_ref[...] + jnp.concatenate([jnp.sin(angle), jnp.cos(angle)], axis=1)
    query = exact_dot(query_tok, dec_qkv_ref[0]) * (LOG2E / math.sqrt(width))
    head_of = iota((slots, 128), 1) // width
    mix = jnp.zeros((slots, 128), f32)
    lev = jnp.zeros((slots, 128), f32)
    for e in range(DEC_HEADS):
        q_high, q_low = split(jnp.where(head_of == e, query, 0.0))
        scores = lax.dot_general(
            jnp.concatenate([q_high, q_high], axis=1), keys[...], contract, preferred_element_type=f32
        ) + lax.dot_general(q_low, keys[:, 0:128], contract, preferred_element_type=f32)
        top = jnp.max(scores, axis=1, keepdims=True)
        weights = jnp.exp2(scores - top)
        total = jnp.sum(weights, axis=1, keepdims=True)
        part = dot(weights.astype(bf16), values[...]) / total
        mix = jnp.where(head_of == e, part, mix)
        lev = jnp.where(head_of == e, top + jnp.log(total) * LOG2E, lev)
    mixed[...] = mix.astype(bf16)
    level[...] = lev

    def stat_copy(kind, d):
        src, dst = ((mixed, got_mixed), (level, got_level))[kind]
        return pltpu.make_async_remote_copy(
            src_ref=src, dst_ref=dst.at[d],
            send_sem=stat_send.at[kind, d], recv_sem=stat_recv.at[kind, d],
            device_id={"tok": lax.rem(me + d, RING)}, device_id_type=MESH,
        )

    for d in (2, 1, 3):
        stat_copy(0, d).start()
        stat_copy(1, d).start()

    gain_col = jnp.sum(
        jnp.where(iota((UP1, UP1), 0) == iota((UP1, UP1), 1), up_gain_ref[...], 0.0), axis=1, keepdims=True
    )
    first_w = up1_ref[...].T.astype(bf16)
    second_w = up2_ref[...].T.astype(bf16)
    lanes = 256

    @pl.loop(0, rows // lanes)
    def _(i):
        span = pl.ds(pl.multiple_of(i * lanes, lanes), lanes)
        wide = lax.dot_general(
            first_w, emb_ref[span, :].astype(bf16), contract, preferred_element_type=f32
        )
        for g in range(4):
            part = wide[g * UP1 : (g + 1) * UP1]
            centred = part - jnp.mean(part, axis=0, keepdims=True)
            spread = jnp.mean(centred * centred, axis=0, keepdims=True)
            first = gelu(centred * lax.rsqrt(spread + 1e-06) * gain_col)
            ups[g, :, span] = gelu(dot(second_w, first.astype(bf16))).astype(bf16)

    for load in late:
        load.wait()
    for d in range(1, RING):
        stat_copy(0, d).wait_recv()
        stat_copy(1, d).wait_recv()
    levels = [lev] + [got_level[d] for d in range(1, RING)]
    parts = [mixed[...].astype(f32)] + [got_mixed[d].astype(f32) for d in range(1, RING)]
    peak = jnp.maximum(jnp.maximum(levels[0], levels[1]), jnp.maximum(levels[2], levels[3]))
    shares = [jnp.exp2(item - peak) for item in levels]
    cross = sum(s * p for s, p in zip(shares, parts)) / sum(shares)

    first_out = norm_rows(
        query_tok + dot(cross.astype(bf16), dec_out_ref[...].astype(bf16)), dec_gains_ref[0:1, :], 1e-05
    )
    hidden = jnp.maximum(dot(first_out.astype(bf16), mlp1[...].astype(bf16)), 0.0)
    second = norm_rows(
        first_out + dot(hidden.astype(bf16), mlp2[...].astype(bf16)), dec_gains_ref[1:2, :], 1e-05
    )
    vec = jnp.maximum(dot(second.astype(bf16), hyper[0].astype(bf16)), 0.0)
    vec = jnp.maximum(dot(vec.astype(bf16), hyper[1].astype(bf16)), 0.0)
    last = hyper_out_ref[...]
    vec = lax.dot_general(
        vec.astype(bf16), jnp.concatenate([last] * 4, axis=0).astype(bf16), contract, preferred_element_type=f32
    ).astype(bf16)
    big = owners * 16
    row = iota((big, slots), 0)
    repeat = (iota((big, slots), 1) == (row // 16) * CAP + row % CAP).astype(bf16)
    row = iota((big, 128), 0)
    stacked = jnp.where((row // CAP) % 4 == iota((big, 128), 1) // UP2, dot(repeat, vec), 0.0).astype(bf16)

    def mask_copy(g, k):
        to = partner(img, k)
        return pltpu.make_async_remote_copy(
            src_ref=ready.at[g, to], dst_ref=received.at[g, img],
            send_sem=mask_send.at[g, k], recv_sem=mask_recv.at[g, k],
            device_id={"img": to}, device_id_type=MESH,
        )

    for g in range(4):
        ready[g] = dot(stacked, ups[g]).astype(bf16).reshape(owners, 16, rows)

        @pl.loop(1, owners)
        def _(k):
            mask_copy(g, lax.rem(k * 13, owners)).start()
        received[g, img] = ready[g, img]

    half = slots // 2
    diagonal = iota((half, half), 0) == iota((half, half), 1)
    spot = jnp.sum(
        jnp.where(diagonal, (place[0] * 16 + place[1]).astype(f32), 0.0), axis=1, keepdims=True
    ).astype(jnp.int32)
    for k in range(4):
        chooser[k * half : (k + 1) * half, :] = (iota((half, owners * 16), 1) == spot + k * CAP).astype(bf16)
    row, col = iota((512, 512), 0), iota((512, 512), 1)
    inside = row % 128
    mover_ref[...] = (col == (inside // GRID) * 256 + (inside % GRID) * 4 + row // 128).astype(bf16)

    @pl.loop(1, owners)
    def _(k):
        point_copy(k).wait_send()
    for d in range(1, RING):
        stat_copy(0, d).wait_send()
        stat_copy(1, d).wait_send()
    for g in range(4):
        @pl.loop(1, owners)
        def _(k):
            mask_copy(g, k).wait_recv()
        chosen_ref[g] = dot(chooser[...], received[g].reshape(owners * 16, rows)).astype(bf16)
    for g in range(4):
        @pl.loop(1, owners)
        def _(k):
            mask_copy(g, k).wait_send()


def trunk(
    picture, ln_gain, w_qkv, w_proj, w_neck1, gain1, w_neck2, gain2, pe_matrix, query_bias, dec_qkv,
    dec_out, dec_gains, w_mlp1, w_mlp2, w_hyper, w_hyper_out, w_up1, up_gain, w_up2, req_image, points, owners,
):
    rows, width = picture.shape
    anywhere = pl.BlockSpec(memory_space=pl.ANY)
    local = pl.BlockSpec(memory_space=pltpu.VMEM)
    inner = HEADS * HDIM
    slots = owners * CAP
    dma = pltpu.SemaphoreType.DMA
    return pl.pallas_call(
        trunk_kernel,
        out_shape=(
            jax.ShapeDtypeStruct((4, slots * 2, rows), bf16),
            jax.ShapeDtypeStruct((512, 512), bf16),
        ),
        in_specs=[anywhere, local, anywhere, anywhere, anywhere, local, anywhere, local]
        + [local] * 7 + [anywhere] * 3 + [local] * 4,
        out_specs=(local, local),
        scratch_shapes=[
            pltpu.VMEM((rows, width), bf16),
            pltpu.VMEM(w_qkv.shape, bf16),
            pltpu.VMEM(w_proj.shape, bf16),
            pltpu.VMEM(w_neck1.shape, bf16),
            pltpu.VMEM(w_neck2.shape, bf16),
            pltpu.VMEM((rows, width), bf16),
            pltpu.VMEM((3 * inner, rows), bf16),
            pltpu.VMEM((3, 2, RING, HDIM, rows), bf16),
            pltpu.VMEM((RING, rows, 128), bf16),
            pltpu.VMEM((2, RING, HDIM, rows), bf16),
            pltpu.VMEM((RING, 2 * HDIM, rows), bf16),
            pltpu.VMEM((3, rows + 2 * GRID, NECK), bf16),
            pltpu.VMEM((2, GRID, NECK), bf16),
            dma((11,)),
            dma((3, 2, RING)),
            dma((3, 2, RING)),
            dma((2, RING)),
            dma((2, RING)),
            dma((2,)),
            dma((2,)),
            pltpu.VMEM((rows, NECK), f32),
            pltpu.VMEM((owners, 8, 128), f32),
            pltpu.VMEM((owners, 8, 128), f32),
            pltpu.VMEM(w_mlp1.shape, f32),
            pltpu.VMEM(w_mlp2.shape, f32),
            pltpu.VMEM(w_hyper.shape, f32),
            pltpu.VMEM((rows, 256), bf16),
            pltpu.VMEM((rows, 128), bf16),
            pltpu.VMEM((slots, 128), bf16),
            pltpu.VMEM((slots, 128), f32),
            pltpu.VMEM((RING, slots, 128), bf16),
            pltpu.VMEM((RING, slots, 128), f32),
            pltpu.VMEM((4, 128, rows), bf16),
            pltpu.VMEM((4, owners, 16, rows), bf16),
            pltpu.VMEM((4, owners, 16, rows), bf16),
            pltpu.VMEM((slots * 2, owners * 16), bf16),
            dma((3,)),
            dma((owners,)),
            dma((owners,)),
            dma((2, RING)),
            dma((2, RING)),
            dma((4, owners)),
            dma((4, owners)),
        ],
        compiler_params=pltpu.CompilerParams(
            collective_id=0, has_side_effects=True, vmem_limit_bytes=62 * 1024 * 1024
        ),
    )(
        picture, ln_gain.reshape(1, -1), w_qkv, w_proj, w_neck1, gain1.reshape(1, -1), w_neck2,
        gain2.reshape(1, -1), req_image.T, points.T, pe_matrix, query_bias.reshape(1, -1), dec_qkv,
        dec_out, dec_gains, w_mlp1, w_mlp2, w_hyper, w_hyper_out.T, w_up1, up_gain.reshape(1, -1), w_up2,
    )


def interleave_kernel(chosen_ref, mover_ref, out_ref):
    slots = out_ref.shape[0]
    sub = chosen_ref.shape[2] // 128
    for p in range(sub):
        span = slice(p * 128, (p + 1) * 128)
        sides = [
            jnp.concatenate(
                [
                    chosen_ref[dr * 2 + dc, (er * 2 + ec) * slots : (er * 2 + ec + 1) * slots, span]
                    for dc in range(2)
                    for ec in range(2)
                ],
                axis=1,
            )
            for dr in range(2)
            for er in range(2)
        ]
        lines = dot(jnp.concatenate(sides, axis=0), mover_ref[...])
        for j in range(4):
            for r in range(2):
                line = (p * 8 + r * 4 + j) * 256
                out_ref[:, line : line + 256] = lines[j * slots : (j + 1) * slots, r * 256 : (r + 1) * 256]


def interleave(chosen, mover):
    groups, tall, rows = chosen.shape
    slots = tall // 4
    lanes = 256
    return pl.pallas_call(
        interleave_kernel,
        out_shape=jax.ShapeDtypeStruct((slots, rows * 16), f32),
        grid=(rows // lanes,),
        in_specs=[
            pl.BlockSpec((groups, tall, lanes), lambda i: (0, 0, i)),
            pl.BlockSpec((512, 512), lambda i: (0, 0)),
        ],
        out_specs=pl.BlockSpec((slots, lanes * 16), lambda i: (0, i)),
        compiler_params=pltpu.CompilerParams(vmem_limit_bytes=56 * 1024 * 1024),
    )(chosen, mover)


def body(tokens, *others):
    return interleave(*trunk(tokens[0], *others, lax.axis_size("img")))


def solution(mesh):
    placed = (
        P("img", "tok", None),
        P(),
        P(),
        P(),
        P(),
        P(),
        P(),
        P(),
        P(),
        P(),
        P(),
        P(),
        P(),
        P(),
        P(),
        P(),
        P(),
        P(),
        P(),
        P(),
        P("img", None),
        P("img", None),
    )
    return jax.shard_map(
        body, mesh=mesh, in_specs=placed, out_specs=P("img", "tok"), check_vma=False
    )
```

profile of v0, /device:TPU:8, one launch (start us, length us, event | category | flops | bytes accessed | tf_op | source)
XLA Modules:
  0.0 152.6 jit_solution(9515192419423465320)
XLA Ops:
  0.0 1.3 reshape.15.gain_ref
  1.3 146.2 %shard_map.208 = (bf16[4,256,1024]{2,1,0:T(8,128)(2,1)}, bf16[512,512]{1,0:T(8,128)(2,1)}) custom-call(bf16[1024,1280]{1,0:T(8,128)(2,1)} %bitcast.8, f32[1,1280]{1,0:T(1,128)} %reshape.15.gain_ref, bf16[1280,1920]{1,0:T(8,128)(2,1)} %wqkv_hbm.1, bf16[640,1280]{1,0:T(8,128)(2,1)} %wproj_hbm.1, bf16[1280,256]{1,0:T(8,128)(2,1)} %wn1_hbm.1, ...), custom_call_target="tpu_custom_call" | custom-call | tf_op jit(solution)/shard_map/pallas_call | solution.py:507
  147.5 5.1 %shard_map.209 = f32[64,16384]{1,0:T(8,128)} custom-call(bf16[4,256,1024]{2,1,0:T(8,128)(2,1)} %get-tuple-element.7.chosen_ref, bf16[512,512]{1,0:T(8,128)(2,1)} %get-tuple-element.8.mover_ref), custom_call_target="tpu_custom_call" | custom-call | tf_op jit(solution)/shard_map/pallas_call | solution.py:599
where the time goes:
time: 155 us; the launch traced here: 153 us
  Pallas kernels  151 us (97%)
    pallas_call x1, Pallas kernels, trunk(): pl.pallas_call(trunk_kernel, out_shape=(jax.ShapeDtypeStruct((4, slots *...  146 us
    pallas_call x1, Pallas kernels, interleave(): pl.pallas_call(interleave_kernel, out_shape=jax.ShapeDtypeStruct((slots,...  5.12 us

commit v1 on v0

--- a/solution.py
+++ b/solution.py
@@ -70,12 +70,12 @@
     tok_hbm, gain_ref, wqkv_hbm, wproj_hbm, wn1_hbm, g1_ref, wn2_hbm, g2_ref,
     req_ref, points_ref, pe_ref, bias_ref, dec_qkv_ref, dec_out_ref, dec_gains_ref,
     mlp1_hbm, mlp2_hbm, hyper_hbm, hyper_out_ref, up1_ref, up_gain_ref, up2_ref,
-    chosen_ref, mover_ref,
+    chosen_hbm, mover_hbm,
     tok, wqkv, wproj, wn1, wn2, normed, loc, got, vrows, outs, att, maps, halo,
     load_sem, qkv_send, qkv_recv, out_send, out_recv, halo_send, halo_recv,
     emb_ref, outgoing, arrived, mlp1, mlp2, hyper, keys, values, mixed, level, got_mixed, got_level, ups,
-    ready, received, chooser,
-    late_sem, point_send, point_recv, stat_send, stat_recv, mask_send, mask_recv,
+    ready, received, chooser, chosen, mover,
+    late_sem, point_send, point_recv, stat_send, stat_recv, mask_send, mask_recv, leave_sem,
 ):
     me = lax.axis_index("tok")
     rows = tok.shape[0]
@@ -91,9 +91,16 @@
         pltpu.make_async_copy(tok_hbm.at[pl.ds(i * tile, tile)], tok.at[pl.ds(i * tile, tile)], load_sem.at[i])
         for i in range(tiles)
     ]
-    loads.append(pltpu.make_async_copy(wqkv_hbm, wqkv, load_sem.at[4]))
+    columns = [pl.ds(kind * inner, inner) for kind in range(3)]
+    weights_in = [
+        pltpu.make_async_copy(wqkv_hbm.at[:, columns[kind]], wqkv.at[:, columns[kind]], load_sem.at[11 + kind])
+        for kind in range(3)
+    ]
+    loads.append(weights_in[1])
     loads.append(pltpu.make_async_copy(wn1_hbm, wn1, load_sem.at[5]))
     loads.append(pltpu.make_async_copy(wn2_hbm, wn2, load_sem.at[6]))
+    loads.append(weights_in[2])
+    loads.append(weights_in[0])
     for d in range(RING):
         owner = lax.rem(me + d, RING)
         loads.append(
@@ -121,12 +128,6 @@
     @pl.loop(1, owners)
     def _(k):
         pl.semaphore_signal(barrier, inc=1, device_id={"img": partner(img, k)}, device_id_type=MESH)
-
-    for i in range(tiles):
-        loads[i].wait()
-        span = pl.ds(i * tile, tile)
-        normed[span, :] = norm_rows(tok[span, :].astype(f32), gain_ref[...], 1e-06).astype(bf16)
-    loads[4].wait()
 
     scale = math.log2(math.e) / math.sqrt(HDIM)
 
@@ -142,8 +143,8 @@
             device_id_type=MESH,
         )
 
-    def project(kind):
-        @pl.loop(0, tiles)
+    def project(kind, first, last):
+        @pl.loop(first, last)
         def _(i):
             span = pl.ds(pl.multiple_of(i * tile, tile), tile)
             part = jnp.dot(
@@ -153,10 +154,34 @@
                 part = part * scale
             loc[kind * inner : (kind + 1) * inner, span] = part.astype(bf16).T
 
-    for kind in (1, 2, 0):
-        project(kind)
-        if kind == 1:
+    def early_keys(d, part):
+        owner = lax.rem(me + d, RING)
+        first = pl.multiple_of(inner + owner * two, 16)
+        span = pl.ds(part * (rows // 2), rows // 2)
+        return pltpu.make_async_remote_copy(
+            src_ref=loc.at[pl.ds(first, HDIM), span],
+            dst_ref=got.at[1, 0, d, :, span],
+            send_sem=qkv_send.at[1, 0, d],
+            recv_sem=qkv_recv.at[1, 0, d],
+            device_id={"tok": owner},
+            device_id_type=MESH,
+        )
+
+    for part in range(2):
+        for i in range(part * tiles // 2, (part + 1) * tiles // 2):
+            loads[i].wait()
+            span = pl.ds(i * tile, tile)
+            normed[span, :] = norm_rows(tok[span, :].astype(f32), gain_ref[...].reshape(1, -1), 1e-06).astype(bf16)
+        if part == 0:
+            weights_in[1].wait()
+        project(1, part * tiles // 2, (part + 1) * tiles // 2)
+        if part == 0:
             pl.semaphore_wait(barrier, owners - 1 + RING - 1)
+        for d in (1, 3, 2):
+            early_keys(d, part).start()
+    for kind in (2, 0):
+        weights_in[kind].wait()
+        project(kind, 0, tiles)
         for d in (1, 3, 2):
             qkv_copy(kind, 0, d).start()
     for kind in (1, 2, 0):
@@ -255,7 +280,7 @@
     for d in range(1, RING):
         for head in range(2):
             out_copy(head, d).wait_recv()
-    for load in loads[5:]:
+    for load in loads[5:7] + loads[9:]:
         load.wait()
 
     def halo_copy(side):
@@ -374,8 +399,10 @@
     head_of = iota((slots, 128), 1) // width
     mix = jnp.zeros((slots, 128), f32)
     lev = jnp.zeros((slots, 128), f32)
-    for e in range(DEC_HEADS):
-        q_high, q_low = split(jnp.where(head_of == e, query, 0.0))
+    group = 4
+    for first in range(0, DEC_HEADS, group):
+        heads = range(first, first + group)
+        q_high, q_low = split(jnp.concatenate([jnp.where(head_of == e, query, 0.0) for e in heads], axis=0))
         scores = lax.dot_general(
             jnp.concatenate([q_high, q_high], axis=1), keys[...], contract, preferred_element_type=f32
         ) + lax.dot_general(q_low, keys[:, 0:128], contract, preferred_element_type=f32)
@@ -383,8 +410,11 @@
         weights = jnp.exp2(scores - top)
         total = jnp.sum(weights, axis=1, keepdims=True)
         part = dot(weights.astype(bf16), values[...]) / total
-        mix = jnp.where(head_of == e, part, mix)
-        lev = jnp.where(head_of == e, top + jnp.log(total) * LOG2E, lev)
+        height = top + jnp.log(total) * LOG2E
+        for j, e in enumerate(heads):
+            at = slice(j * slots, (j + 1) * slots)
+            mix = jnp.where(head_of == e, part[at], mix)
+            lev = jnp.where(head_of == e, height[at], lev)
     mixed[...] = mix.astype(bf16)
     level[...] = lev
 
@@ -475,7 +505,7 @@
         chooser[k * half : (k + 1) * half, :] = (iota((half, owners * 16), 1) == spot + k * CAP).astype(bf16)
     row, col = iota((512, 512), 0), iota((512, 512), 1)
     inside = row % 128
-    mover_ref[...] = (col == (inside // GRID) * 256 + (inside % GRID) * 4 + row // 128).astype(bf16)
+    mover[...] = (col == (inside // GRID) * 256 + (inside % GRID) * 4 + row // 128).astype(bf16)
 
     @pl.loop(1, owners)
     def _(k):
@@ -483,15 +513,21 @@
     for d in range(1, RING):
         stat_copy(0, d).wait_send()
         stat_copy(1, d).wait_send()
+    leaving = [pltpu.make_async_copy(mover, mover_hbm, leave_sem.at[4])]
+    leaving[0].start()
     for g in range(4):
         @pl.loop(1, owners)
         def _(k):
             mask_copy(g, k).wait_recv()
-        chosen_ref[g] = dot(chooser[...], received[g].reshape(owners * 16, rows)).astype(bf16)
+        chosen[g] = dot(chooser[...], received[g].reshape(owners * 16, rows)).astype(bf16)
+        leaving.append(pltpu.make_async_copy(chosen.at[g], chosen_hbm.at[g], leave_sem.at[g]))
+        leaving[-1].start()
     for g in range(4):
         @pl.loop(1, owners)
         def _(k):
             mask_copy(g, k).wait_send()
+    for copy in leaving:
+        copy.wait()
 
 
 def trunk(
@@ -512,7 +548,7 @@
         ),
         in_specs=[anywhere, local, anywhere, anywhere, anywhere, local, anywhere, local]
         + [local] * 7 + [anywhere] * 3 + [local] * 4,
-        out_specs=(local, local),
+        out_specs=(anywhere, anywhere),
         scratch_shapes=[
             pltpu.VMEM((rows, width), bf16),
             pltpu.VMEM(w_qkv.shape, bf16),
@@ -527,7 +563,7 @@
             pltpu.VMEM((RING, 2 * HDIM, rows), bf16),
             pltpu.VMEM((3, rows + 2 * GRID, NECK), bf16),
             pltpu.VMEM((2, GRID, NECK), bf16),
-            dma((11,)),
+            dma((14,)),
             dma((3, 2, RING)),
             dma((3, 2, RING)),
             dma((2, RING)),
@@ -550,6 +586,8 @@
             pltpu.VMEM((4, owners, 16, rows), bf16),
             pltpu.VMEM((4, owners, 16, rows), bf16),
             pltpu.VMEM((slots * 2, owners * 16), bf16),
+            pltpu.VMEM((4, slots * 2, rows), bf16),
+            pltpu.VMEM((512, 512), bf16),
             dma((3,)),
             dma((owners,)),
             dma((owners,)),
@@ -557,12 +595,13 @@
             dma((2, RING)),
             dma((4, owners)),
             dma((4, owners)),
+            dma((5,)),
         ],
         compiler_params=pltpu.CompilerParams(
             collective_id=0, has_side_effects=True, vmem_limit_bytes=62 * 1024 * 1024
         ),
     )(
-        picture, ln_gain.reshape(1, -1), w_qkv, w_proj, w_neck1, gain1.reshape(1, -1), w_neck2,
+        picture, ln_gain, w_qkv, w_proj, w_neck1, gain1.reshape(1, -1), w_neck2,
         gain2.reshape(1, -1), req_image.T, points.T, pe_matrix, query_bias.reshape(1, -1), dec_qkv,
         dec_out, dec_gains, w_mlp1, w_mlp2, w_hyper, w_hyper_out.T, w_up1, up_gain.reshape(1, -1), w_up2,
     )
@@ -571,25 +610,28 @@
 def interleave_kernel(chosen_ref, mover_ref, out_ref):
     slots = out_ref.shape[0]
     sub = chosen_ref.shape[2] // 128
+    sides = [
+        jnp.concatenate(
+            [
+                chosen_ref[
+                    dr * 2 + dc, (er * 2 + ec) * slots : (er * 2 + ec + 1) * slots, p * 128 : (p + 1) * 128
+                ]
+                for dc in range(2)
+                for ec in range(2)
+            ],
+            axis=1,
+        )
+        for p in range(sub)
+        for dr in range(2)
+        for er in range(2)
+    ]
+    lines = dot(jnp.concatenate(sides, axis=0), mover_ref[...])
     for p in range(sub):
-        span = slice(p * 128, (p + 1) * 128)
-        sides = [
-            jnp.concatenate(
-                [
-                    chosen_ref[dr * 2 + dc, (er * 2 + ec) * slots : (er * 2 + ec + 1) * slots, span]
-                    for dc in range(2)
-                    for ec in range(2)
-                ],
-                axis=1,
-            )
-            for dr in range(2)
-            for er in range(2)
-        ]
-        lines = dot(jnp.concatenate(sides, axis=0), mover_ref[...])
         for j in range(4):
+            at = slice((p * 4 + j) * slots, (p * 4 + j + 1) * slots)
             for r in range(2):
                 line = (p * 8 + r * 4 + j) * 256
-                out_ref[:, line : line + 256] = lines[j * slots : (j + 1) * slots, r * 256 : (r + 1) * 256]
+                out_ref[:, line : line + 256] = lines[at, r * 256 : (r + 1) * 256]
 
 
 def interleave(chosen, mover):

time: 155 us -> 149 us (0.961)
  Pallas kernels: 151 us -> 147 us
    pallas_call x1, Pallas kernels: 146 us -> 142 us  [trunk(): pl.pallas_call(trunk_kernel, out_shape=(jax.ShapeDtypeStruct((4, slots *...]
where the time goes in v1:
time: 149 us; the launch traced here: 147 us
  Pallas kernels  147 us (99%)
    pallas_call x1, Pallas kernels, trunk(): pl.pallas_call(trunk_kernel, out_shape=(jax.ShapeDtypeStruct((4, slots *...  142 us
    pallas_call x1, Pallas kernels, interleave(): pl.pallas_call(interleave_kernel, out_shape=jax.ShapeDtypeStruct((slots,...  5.12 us

profile of v1, /device:TPU:8, one launch (start us, length us, event | category | flops | bytes accessed | tf_op | source)
XLA Modules:
  0.0 146.9 jit_solution(425738316216019675)
XLA Ops:
  0.0 141.8 %shard_map.208 = (bf16[4,256,1024]{2,1,0:T(8,128)(2,1)}, bf16[512,512]{1,0:T(8,128)(2,1)}) custom-call(bf16[1024,1280]{1,0:T(8,128)(2,1)} %bitcast.8, f32[1280]{0:T(1024)} %gain_ref.1, bf16[1280,1920]{1,0:T(8,128)(2,1)} %wqkv_hbm.1, bf16[640,1280]{1,0:T(8,128)(2,1)} %wproj_hbm.1, bf16[1280,256]{1,0:T(8,128)(2,1)} %wn1_hbm.1, f32[1,256]{1,0:T(1,128)} %bitcast.10, ...), custom_call_target="tpu_custom_call" | custom-call | tf_op jit(solution)/shard_map/pallas_call | solution.py:543
  141.8 5.1 %shard_map.209 = f32[64,16384]{1,0:T(8,128)} custom-call(bf16[4,256,1024]{2,1,0:T(8,128)(2,1)} %get-tuple-element.7.chosen_ref, bf16[512,512]{1,0:T(8,128)(2,1)} %get-tuple-element.8.mover_ref), custom_call_target="tpu_custom_call" | custom-call | tf_op jit(solution)/shard_map/pallas_call | solution.py:641

commit v2 on v1

--- a/solution.py
+++ b/solution.py
@@ -368,19 +368,19 @@
     key_w = dec_qkv_ref[1]
     value_w = dec_qkv_ref[2].astype(bf16)
     key_high, key_low = split(key_w)
+    codes = []
     for r in range(grid_rows):
-        span = pl.ds(r * GRID, GRID)
         rs, rc = row_sin[r : r + 1], row_cos[r : r + 1]
-        code = jnp.concatenate(
-            [col_sin * rc + col_cos * rs, col_cos * rc - col_sin * rs], axis=1
-        )
-        cell = emb_ref[span, :]
-        high, low = split(cell + code)
-        projected = dot(high, key_high) + (dot(high, key_low) + dot(low, key_high))
-        k_high, k_low = split(projected)
-        keys[span, 0:128] = k_high
-        keys[span, 128:256] = k_low
-        values[span, :] = dot(cell.astype(bf16), value_w).astype(bf16)
+        codes.append(
+            jnp.concatenate([col_sin * rc + col_cos * rs, col_cos * rc - col_sin * rs], axis=1)
+        )
+    cell = emb_ref[...]
+    high, low = split(cell + jnp.concatenate(codes, axis=0))
+    both = dot(high, jnp.concatenate([key_high, key_low], axis=1))
+    k_high, k_low = split(both[:, 0:128] + (both[:, 128:256] + dot(low, key_high)))
+    keys[:, 0:128] = k_high
+    keys[:, 128:256] = k_low
+    values[...] = dot(cell.astype(bf16), value_w).astype(bf16)
 
     @pl.loop(1, owners)
     def _(k):
@@ -452,6 +452,8 @@
 
     for load in late:
         load.wait()
+    mlp1_w, mlp2_w = mlp1[...].astype(bf16), mlp2[...].astype(bf16)
+    hyper_w = [hyper[i].astype(bf16) for i in range(2)]
     for d in range(1, RING):
         stat_copy(0, d).wait_recv()
         stat_copy(1, d).wait_recv()
@@ -464,12 +466,12 @@
     first_out = norm_rows(
         query_tok + dot(cross.astype(bf16), dec_out_ref[...].astype(bf16)), dec_gains_ref[0:1, :], 1e-05
     )
-    hidden = jnp.maximum(dot(first_out.astype(bf16), mlp1[...].astype(bf16)), 0.0)
+    hidden = jnp.maximum(dot(first_out.astype(bf16), mlp1_w), 0.0)
     second = norm_rows(
-        first_out + dot(hidden.astype(bf16), mlp2[...].astype(bf16)), dec_gains_ref[1:2, :], 1e-05
-    )
-    vec = jnp.maximum(dot(second.astype(bf16), hyper[0].astype(bf16)), 0.0)
-    vec = jnp.maximum(dot(vec.astype(bf16), hyper[1].astype(bf16)), 0.0)
+        first_out + dot(hidden.astype(bf16), mlp2_w), dec_gains_ref[1:2, :], 1e-05
+    )
+    vec = jnp.maximum(dot(second.astype(bf16), hyper_w[0]), 0.0)
+    vec = jnp.maximum(dot(vec.astype(bf16), hyper_w[1]), 0.0)
     last = hyper_out_ref[...]
     vec = lax.dot_general(
         vec.astype(bf16), jnp.concatenate([last] * 4, axis=0).astype(bf16), contract, preferred_element_type=f32

time: 149 us -> 149 us (level)
  no operation moved by 1% of the time
where the time goes in v2:
time: 149 us; the launch traced here: 147 us
  Pallas kernels  147 us (99%)
    pallas_call x1, Pallas kernels, trunk(): pl.pallas_call(trunk_kernel, out_shape=(jax.ShapeDtypeStruct((4, slots *...  142 us
    pallas_call x1, Pallas kernels, interleave(): pl.pallas_call(interleave_kernel, out_shape=jax.ShapeDtypeStruct((slots,...  5.12 us

profile of v2, /device:TPU:8, one launch (start us, length us, event | category | flops | bytes accessed | tf_op | source)
XLA Modules:
  0.0 147.1 jit_solution(12844263139188659883)
XLA Ops:
  0.0 142.0 %shard_map.208 = (bf16[4,256,1024]{2,1,0:T(8,128)(2,1)}, bf16[512,512]{1,0:T(8,128)(2,1)}) custom-call(bf16[1024,1280]{1,0:T(8,128)(2,1)} %bitcast.8, f32[1280]{0:T(1024)} %gain_ref.1, bf16[1280,1920]{1,0:T(8,128)(2,1)} %wqkv_hbm.1, bf16[640,1280]{1,0:T(8,128)(2,1)} %wproj_hbm.1, bf16[1280,256]{1,0:T(8,128)(2,1)} %wn1_hbm.1, f32[1,256]{1,0:T(1,128)} %bitcast.10, ...), custom_call_target="tpu_custom_call" | custom-call | tf_op jit(solution)/shard_map/pallas_call | solution.py:545
  142.0 5.1 %shard_map.209 = f32[64,16384]{1,0:T(8,128)} custom-call(bf16[4,256,1024]{2,1,0:T(8,128)(2,1)} %get-tuple-element.7.chosen_ref, bf16[512,512]{1,0:T(8,128)(2,1)} %get-tuple-element.8.mover_ref), custom_call_target="tpu_custom_call" | custom-call | tf_op jit(solution)/shard_map/pallas_call | solution.py:643
